TPU v7x, 128 devices: a whole 4x4x4 slice. The times are simulated.
128 devices in a mesh: query: 8 (over x, z_hi), tok: 16 (over y, z_lo, core).
Axes of the slice: x: 4, y: 4, z: 4 (z_hi: 2, z_lo: 2; z = z_hi * 2 + z_lo), core: 2. Of those that a mesh axis runs over, the one named last changes fastest.
Arguments:
- queries: bfloat16 [32768, 128], P('query'), may hold values from -16 to 16, as said below
- documents: bfloat16 [32768, 128], P('tok'), may hold values from -10 to 10, as said below
- cotangent: float32 [1024], P('query'), may hold values from -6 to 6
Outputs:
- grad_queries: float32 [32768, 128], P(('query', 'tok'))
- grad_documents: float32 [16, 2048, 128], P('tok', 'query')
Inputs may be any that keep to these rules, and one draw needn't show every extreme that they name: `documents`: document embeddings of order one. `queries`: query embeddings of order one.
All inputs are finite; a program needn't handle non-finite values.
Results may differ from a plain program's by a relative error of at most 0.0029.
Values may be sent and summed in bfloat16 or wider, within the bound.
A program may use at most 64 MiB of HBM per device.

v0:
```python
import jax
import jax.numpy as jnp
from jax import lax
from jax.sharding import PartitionSpec as P

QLEN = 32
inv_temp = 2.0


def score_rows(q_rows, doc_rows):
    return (
        lax.dot_general(
            q_rows, doc_rows, (((1,), (1,)), ((), ())), preferred_element_type=jnp.float32
        )
        * inv_temp
    )


def shards(queries, documents, cotangent):
    n_rows, feat_width = queries.shape
    n_docs = documents.shape[0]
    blk_rows = min(512, n_rows)
    n_blocks = n_rows // blk_rows
    row_weight = jnp.broadcast_to(cotangent[:, None], (cotangent.shape[0], QLEN)).reshape(-1)
    q_blocks = queries.reshape(n_blocks, blk_rows, feat_width)

    def local_stats(carry, q_rows):
        scores = score_rows(q_rows, documents)
        row_top = jnp.max(scores, axis=1)
        row_total = jnp.sum(jnp.exp(scores - row_top[:, None]), axis=1)
        return (carry, (row_top, row_total))

    _, (row_tops, row_totals) = lax.scan(local_stats, 0, q_blocks)
    row_tops = row_tops.reshape(-1)
    row_totals = row_totals.reshape(-1)
    top_all = lax.pmax(row_tops, "tok")
    total_all = lax.psum(row_totals * jnp.exp(row_tops - top_all), "tok")
    log_total = top_all + jnp.log(total_all)
    log_blocks = log_total.reshape(n_blocks, blk_rows)
    weight_blocks = row_weight.reshape(n_blocks, blk_rows)

    def backward_both(doc_total, inputs_blk):
        q_rows, log_rows, weight_rows = inputs_blk
        scores = score_rows(q_rows, documents)
        probs = jnp.exp(scores - log_rows[:, None])
        weights_low = probs.astype(jnp.bfloat16)
        grad_rows = weight_rows[:, None] * jnp.dot(
            weights_low, documents, preferred_element_type=jnp.float32
        )
        scaled = (weight_rows[:, None] * probs).astype(jnp.bfloat16)
        doc_total = doc_total + lax.dot_general(
            scaled, q_rows, (((0,), (0,)), ((), ())), preferred_element_type=jnp.float32
        )
        return (doc_total, grad_rows)

    doc_total, grad_blocks = lax.scan(
        backward_both,
        jnp.zeros((n_docs, feat_width), jnp.float32),
        (q_blocks, log_blocks, weight_blocks),
    )
    grad_docs = lax.psum_scatter(doc_total, "query", scatter_dimension=0, tiled=True)
    query_terms = grad_blocks.reshape(n_rows, feat_width)
    grad_q = lax.psum_scatter(query_terms, "tok", scatter_dimension=0, tiled=True)
    return (grad_q, grad_docs[None])


def solution(mesh):
    placed = (P("query", None), P("tok", None), P("query"))
    return jax.shard_map(
        shards,
        mesh=mesh,
        in_specs=placed,
        out_specs=(P(("query", "tok"), None), P("tok", "query", None)),
        check_vma=False,
    )
```

profile of v0, /device:TPU:0, one launch (start us, length us, event | category | flops | bytes accessed | tf_op | source)
XLA Modules:
  0.0 358.9 jit_solution(10717387732099525368)
XLA Ops:
  7.3 23.1 %while.25 = (s32[]{:T(128)}, f32[8,512]{1,0:T(8,128)S(1)}, f32[8,512]{1,0:T(8,128)S(1)}, bf16[8,512,128]{2,1,0:T(8,128)(2,1)}, bf16[2048,128]{1,0:T(8,128)(2,1)}, /*index=5*/s32[]{:T(128)}, s32[]{:T(128)}) while((s32[]{:T(128)}, f32[8,512]{1,0:T(8,128)S(1)}, f32[8,512]{1,0:T(8,128)S(1)}, bf16[8,512,128]{2,1,0:T(8,128)(2,1)}, ...), condition=%wide.region_3.4_spmd, body=%wide.region_0.3_spmd.sunk | while | flops 273677312 | bytes 9058901 | solution.py:33
  7.3 1.9 multiply_reduce_fusion.2
  10.2 1.9 multiply_reduce_fusion.2
  13.0 1.9 multiply_reduce_fusion.2
  15.9 1.9 multiply_reduce_fusion.2
  18.8 1.9 multiply_reduce_fusion.2
  21.7 1.9 multiply_reduce_fusion.2
  24.6 1.9 multiply_reduce_fusion.2
  27.4 1.9 multiply_reduce_fusion.2
  30.3 56.7 %pmax.7 = f32[4096]{0:T(1024)S(1)} all-reduce(f32[4096]{0:T(1024)S(1)} %bitcast.57), channel_id=1, replica_groups=mesh['query'=8,'tok'=16] {'tok'}, use_global_device_ids=true, to_apply=%region_4.5 | all-reduce | flops 4096 | bytes 32768 | tf_op jit(solution)/shard_map/pmax | solution.py:36
  87.0 52.9 %psum.7 = f32[4096]{0:T(1024)S(1)} all-reduce(f32[4096]{0:T(1024)S(1)} %exponential_multiply_fusion), channel_id=1, replica_groups=mesh['query'=8,'tok'=16] {'tok'}, use_global_device_ids=true, to_apply=%region_5.6 | all-reduce | flops 4096 | bytes 32768 | tf_op jit(solution)/shard_map/psum | solution.py:37
  140.2 72.0 %while.26 = (s32[]{:T(128)}, f32[2048,128]{1,0:T(8,128)S(1)}, f32[8,512,128]{2,1,0:T(8,128)}, f32[8,512]{1,0:T(8,128)S(1)}, bf16[8,512,128]{2,1,0:T(8,128)(2,1)}...) while((s32[]{:T(128)}, f32[2048,128]{1,0:T(8,128)S(1)}, ...), condition=%wide.region_7.8_spmd.clone, body=%wide.region_6.7_spmd.clone.sunk | while | flops 813236224 | bytes 35145376 | solution.py:56
  142.1 1.9 copy-done
  145.6 3.6 %convolution_add_fusion.2 = f32[2048,128]{1,0:T(8,128)S(1)} fusion(f32[512,2048]{1,0:T(8,128)} %copy-done, f32[512]{0:T(512)S(1)} %bitcast.53, f32[512]{0:T(512)S(1)} %bitcast.55, f32[2048,128]{1,0:T(8,128)S(1)} %get-tuple-element.237, pred[]{:T(512)S(6)} %compare.3, bf16[8,512,128]{2,1,0:T(8,128)(2,1)} %get-tuple-element.249, s32[]{:T(128)} %get-tuple-element.236), kind=kOutput, calls=%fused_computation.9.clone.1 | convolution fusion | flops 273154048 | bytes 6427137 | tf_op jit(solution)/shard_map/while/body/eval_jaxpr/dot_general | solution.py:51
  151.1 1.9 copy-done
  154.6 3.6 %convolution_add_fusion.2 = f32[2048,128]{1,0:T(8,128)S(1)} fusion(f32[512,2048]{1,0:T(8,128)} %copy-done, f32[512]{0:T(512)S(1)} %bitcast.53, f32[512]{0:T(512)S(1)} %bitcast.55, f32[2048,128]{1,0:T(8,128)S(1)} %get-tuple-element.237, pred[]{:T(512)S(6)} %compare.3, bf16[8,512,128]{2,1,0:T(8,128)(2,1)} %get-tuple-element.249, s32[]{:T(128)} %get-tuple-element.236), kind=kOutput, calls=%fused_computation.9.clone.1 | convolution fusion | flops 273154048 | bytes 6427137 | tf_op jit(solution)/shard_map/while/body/eval_jaxpr/dot_general | solution.py:51
  163.6 3.6 %convolution_add_fusion.2 = f32[2048,128]{1,0:T(8,128)S(1)} fusion(f32[512,2048]{1,0:T(8,128)} %copy-done, f32[512]{0:T(512)S(1)} %bitcast.53, f32[512]{0:T(512)S(1)} %bitcast.55, f32[2048,128]{1,0:T(8,128)S(1)} %get-tuple-element.237, pred[]{:T(512)S(6)} %compare.3, bf16[8,512,128]{2,1,0:T(8,128)(2,1)} %get-tuple-element.249, s32[]{:T(128)} %get-tuple-element.236), kind=kOutput, calls=%fused_computation.9.clone.1 | convolution fusion | flops 273154048 | bytes 6427137 | tf_op jit(solution)/shard_map/while/body/eval_jaxpr/dot_general | solution.py:51
  172.6 3.6 %convolution_add_fusion.2 = f32[2048,128]{1,0:T(8,128)S(1)} fusion(f32[512,2048]{1,0:T(8,128)} %copy-done, f32[512]{0:T(512)S(1)} %bitcast.53, f32[512]{0:T(512)S(1)} %bitcast.55, f32[2048,128]{1,0:T(8,128)S(1)} %get-tuple-element.237, pred[]{:T(512)S(6)} %compare.3, bf16[8,512,128]{2,1,0:T(8,128)(2,1)} %get-tuple-element.249, s32[]{:T(128)} %get-tuple-element.236), kind=kOutput, calls=%fused_computation.9.clone.1 | convolution fusion | flops 273154048 | bytes 6427137 | tf_op jit(solution)/shard_map/while/body/eval_jaxpr/dot_general | solution.py:51
  181.6 3.6 %convolution_add_fusion.2 = f32[2048,128]{1,0:T(8,128)S(1)} fusion(f32[512,2048]{1,0:T(8,128)} %copy-done, f32[512]{0:T(512)S(1)} %bitcast.53, f32[512]{0:T(512)S(1)} %bitcast.55, f32[2048,128]{1,0:T(8,128)S(1)} %get-tuple-element.237, pred[]{:T(512)S(6)} %compare.3, bf16[8,512,128]{2,1,0:T(8,128)(2,1)} %get-tuple-element.249, s32[]{:T(128)} %get-tuple-element.236), kind=kOutput, calls=%fused_computation.9.clone.1 | convolution fusion | flops 273154048 | bytes 6427137 | tf_op jit(solution)/shard_map/while/body/eval_jaxpr/dot_general | solution.py:51
  190.6 3.6 %convolution_add_fusion.2 = f32[2048,128]{1,0:T(8,128)S(1)} fusion(f32[512,2048]{1,0:T(8,128)} %copy-done, f32[512]{0:T(512)S(1)} %bitcast.53, f32[512]{0:T(512)S(1)} %bitcast.55, f32[2048,128]{1,0:T(8,128)S(1)} %get-tuple-element.237, pred[]{:T(512)S(6)} %compare.3, bf16[8,512,128]{2,1,0:T(8,128)(2,1)} %get-tuple-element.249, s32[]{:T(128)} %get-tuple-element.236), kind=kOutput, calls=%fused_computation.9.clone.1 | convolution fusion | flops 273154048 | bytes 6427137 | tf_op jit(solution)/shard_map/while/body/eval_jaxpr/dot_general | solution.py:51
  199.6 3.6 %convolution_add_fusion.2 = f32[2048,128]{1,0:T(8,128)S(1)} fusion(f32[512,2048]{1,0:T(8,128)} %copy-done, f32[512]{0:T(512)S(1)} %bitcast.53, f32[512]{0:T(512)S(1)} %bitcast.55, f32[2048,128]{1,0:T(8,128)S(1)} %get-tuple-element.237, pred[]{:T(512)S(6)} %compare.3, bf16[8,512,128]{2,1,0:T(8,128)(2,1)} %get-tuple-element.249, s32[]{:T(128)} %get-tuple-element.236), kind=kOutput, calls=%fused_computation.9.clone.1 | convolution fusion | flops 273154048 | bytes 6427137 | tf_op jit(solution)/shard_map/while/body/eval_jaxpr/dot_general | solution.py:51
  208.6 3.6 %convolution_add_fusion.2 = f32[2048,128]{1,0:T(8,128)S(1)} fusion(f32[512,2048]{1,0:T(8,128)} %copy-done, f32[512]{0:T(512)S(1)} %bitcast.53, f32[512]{0:T(512)S(1)} %bitcast.55, f32[2048,128]{1,0:T(8,128)S(1)} %get-tuple-element.237, pred[]{:T(512)S(6)} %compare.3, bf16[8,512,128]{2,1,0:T(8,128)(2,1)} %get-tuple-element.249, s32[]{:T(128)} %get-tuple-element.236), kind=kOutput, calls=%fused_computation.9.clone.1 | convolution fusion | flops 273154048 | bytes 6427137 | tf_op jit(solution)/shard_map/while/body/eval_jaxpr/dot_general | solution.py:51
  214.0 71.5 %reduce-scatter.5.cloned.1.call-done = f32[256,128]{1,0:T(8,128)} async-done(((f32[2048,128]{1,0:T(8,128)}), f32[256,128]{1,0:T(8,128)}) %reduce-scatter.5.cloned.1.call-update) | async-done | bytes 131088 | tf_op jit(solution)/shard_map/reduce_scatter | solution.py:61
  285.5 66.6 %reduce-scatter.3.cloned.1.call-done = f32[256,128]{1,0:T(8,128)} async-done(((f32[4096,128]{1,0:T(8,128)}), f32[256,128]{1,0:T(8,128)}) %reduce-scatter.3.cloned.1.call-update) | async-done | bytes 131088 | tf_op jit(solution)/shard_map/reduce_scatter | solution.py:63
  (98 shorter events, 48.5 us)
Async XLA Ops:
  7.2 278.3 %reduce-scatter.5.cloned.1.call-start = ((), (), s32[]{:S(2)}) async-start(), calls=%async_computation.3 | async-start | bytes 1179648 | tf_op jit(solution)/shard_map/reduce_scatter | solution.py:61
  7.2 132.7 %copy-start.3 = (f32[128]{0:T(128)S(1)}, f32[128]{0:T(128)}, u32[]{:S(2)}) copy-start(f32[128]{0:T(128)} %param.9) | copy-start | bytes 1540
  140.2 3.8 %copy-start.1 = (bf16[2048,128]{1,0:T(8,128)(2,1)S(1)}, bf16[2048,128]{1,0:T(8,128)(2,1)}, u32[]{:S(2)}) copy-start(bf16[2048,128]{1,0:T(8,128)(2,1)} %get-tuple-element.250) | copy-start | bytes 1572868 | tf_op jit(solution)/shard_map/while
  142.1 1.9 copy-start
  149.2 3.8 %copy-start.1 = (bf16[2048,128]{1,0:T(8,128)(2,1)S(1)}, bf16[2048,128]{1,0:T(8,128)(2,1)}, u32[]{:S(2)}) copy-start(bf16[2048,128]{1,0:T(8,128)(2,1)} %get-tuple-element.250) | copy-start | bytes 1572868 | tf_op jit(solution)/shard_map/while
  151.1 1.9 copy-start
  158.2 3.8 %copy-start.1 = (bf16[2048,128]{1,0:T(8,128)(2,1)S(1)}, bf16[2048,128]{1,0:T(8,128)(2,1)}, u32[]{:S(2)}) copy-start(bf16[2048,128]{1,0:T(8,128)(2,1)} %get-tuple-element.250) | copy-start | bytes 1572868 | tf_op jit(solution)/shard_map/while
  160.1 1.9 copy-start
  167.2 3.8 %copy-start.1 = (bf16[2048,128]{1,0:T(8,128)(2,1)S(1)}, bf16[2048,128]{1,0:T(8,128)(2,1)}, u32[]{:S(2)}) copy-start(bf16[2048,128]{1,0:T(8,128)(2,1)} %get-tuple-element.250) | copy-start | bytes 1572868 | tf_op jit(solution)/shard_map/while
  169.1 1.9 copy-start
  176.2 3.8 %copy-start.1 = (bf16[2048,128]{1,0:T(8,128)(2,1)S(1)}, bf16[2048,128]{1,0:T(8,128)(2,1)}, u32[]{:S(2)}) copy-start(bf16[2048,128]{1,0:T(8,128)(2,1)} %get-tuple-element.250) | copy-start | bytes 1572868 | tf_op jit(solution)/shard_map/while
  178.1 1.9 copy-start
  185.2 3.8 %copy-start.1 = (bf16[2048,128]{1,0:T(8,128)(2,1)S(1)}, bf16[2048,128]{1,0:T(8,128)(2,1)}, u32[]{:S(2)}) copy-start(bf16[2048,128]{1,0:T(8,128)(2,1)} %get-tuple-element.250) | copy-start | bytes 1572868 | tf_op jit(solution)/shard_map/while
  187.1 1.9 copy-start
  194.2 3.8 %copy-start.1 = (bf16[2048,128]{1,0:T(8,128)(2,1)S(1)}, bf16[2048,128]{1,0:T(8,128)(2,1)}, u32[]{:S(2)}) copy-start(bf16[2048,128]{1,0:T(8,128)(2,1)} %get-tuple-element.250) | copy-start | bytes 1572868 | tf_op jit(solution)/shard_map/while
  196.1 1.9 copy-start
  203.2 3.8 %copy-start.1 = (bf16[2048,128]{1,0:T(8,128)(2,1)S(1)}, bf16[2048,128]{1,0:T(8,128)(2,1)}, u32[]{:S(2)}) copy-start(bf16[2048,128]{1,0:T(8,128)(2,1)} %get-tuple-element.250) | copy-start | bytes 1572868 | tf_op jit(solution)/shard_map/while
  205.1 1.9 copy-start
  212.2 1.0 copy-start.2
  213.2 138.9 %reduce-scatter.3.cloned.1.call-start = ((), (), s32[]{:S(2)}) async-start(), calls=%async_computation.2 | async-start | bytes 2228224 | tf_op jit(solution)/shard_map/reduce_scatter | solution.py:63
Sparse Core Ops, SparseCore 0:
  213.4 72.0 reduce-scatter.4
  288.4 63.6 reduce-scatter.2
where the time goes:
time: 359 us
  waiting for transfers between devices  139 us (39%)
  blocking collectives  110 us (31%)
  matrix products  71.5 us (20%)
  local copies, waits for them, and re-layouts  17.5 us (5%)
  between operations  14.1 us (4%)
  other arithmetic  6.62 us (2%)
    reduce_scatter x1, waiting for transfers between devices, shards(): lax.psum_scatter(doc_total, 'query', scatter_dimension=0, tiled=True)  71.5 us
    reduce_scatter x1, waiting for transfers between devices, shards(): lax.psum_scatter(query_terms, 'tok', scatter_dimension=0, tiled=True)  66.6 us
    pmax x1, blocking collectives, shards(): top_all = lax.pmax(row_tops, 'tok')  56.7 us
    psum x1, blocking collectives, shards(): total_all = lax.psum(row_totals * jnp.exp(row_tops - top_all), 'tok')  52.9 us
    dot_general x16, matrix products, score_rows(): lax.dot_general(q_rows, doc_rows, (((1,), (1,)), ((), ())), preferred_ele...  30.2 us
    dot_general x8, matrix products, backward_both(): lax.dot_general(scaled, q_rows, (((0,), (0,)), ((), ())), preferred_eleme...  28.9 us
    while x32, local copies, waits for them, and re-layouts  15.2 us
    dot_general x8, matrix products, backward_both(): jnp.dot(weights_low, documents, preferred_element_type=jnp.float32)  12.4 us
  transfers between devices with their start and end apart: 2, of which 2 were waited for; matrix products, arithmetic and copies ran while one was open for 0% of the time, Pallas kernels for 0%

commit v1 on v0

--- a/solution.py
+++ b/solution.py
@@ -34,7 +34,9 @@
     row_tops = row_tops.reshape(-1)
     row_totals = row_totals.reshape(-1)
     top_all = lax.pmax(row_tops, "tok")
-    total_all = lax.psum(row_totals * jnp.exp(row_tops - top_all), "tok")
+    part = row_totals * jnp.exp(row_tops - top_all)
+    shards_2 = lax.all_gather(part, "tok")
+    total_all = jnp.sum(shards_2, axis=0)
     log_total = top_all + jnp.log(total_all)
     log_blocks = log_total.reshape(n_blocks, blk_rows)
     weight_blocks = row_weight.reshape(n_blocks, blk_rows)

time: 359 us -> 324 us (0.903)
  blocking collectives: 110 us -> 73.3 us
    psum x1 -> x0, blocking collectives: 52.9 us -> none  [shards(): total_all = lax.psum(row_totals * jnp.exp(row_tops - top_all), 'tok')]
    all_gather x0 -> x1, blocking collectives: none -> 16.7 us  [shards(): shards_2 = lax.all_gather(part, 'tok')]
where the time goes in v1:
time: 324 us; the launch traced here: 323 us
  waiting for transfers between devices  139 us (43%)
  blocking collectives  73.3 us (23%)
  matrix products  71.5 us (22%)
  local copies, waits for them, and re-layouts  17.6 us (5%)
  between operations  14.1 us (4%)
  other arithmetic  6.66 us (2%)
    reduce_scatter x1, waiting for transfers between devices, shards(): lax.psum_scatter(doc_total, 'query', scatter_dimension=0, tiled=True)  72 us
    reduce_scatter x1, waiting for transfers between devices, shards(): lax.psum_scatter(query_terms, 'tok', scatter_dimension=0, tiled=True)  66.4 us
    pmax x1, blocking collectives, shards(): top_all = lax.pmax(row_tops, 'tok')  56.7 us
    dot_general x16, matrix products, score_rows(): lax.dot_general(q_rows, doc_rows, (((1,), (1,)), ((), ())), preferred_ele...  30.2 us
    dot_general x8, matrix products, backward_both(): lax.dot_general(scaled, q_rows, (((0,), (0,)), ((), ())), preferred_eleme...  28.9 us
    all_gather x1, blocking collectives, shards(): shards_2 = lax.all_gather(part, 'tok')  16.7 us
    while x32, local copies, waits for them, and re-layouts  15.2 us
    dot_general x8, matrix products, backward_both(): jnp.dot(weights_low, documents, preferred_element_type=jnp.float32)  12.4 us
  transfers between devices with their start and end apart: 2, of which 2 were waited for; matrix products, arithmetic and copies ran while one was open for 0% of the time, Pallas kernels for 0%

profile of v1, /device:TPU:0, one launch (start us, length us, event | category | flops | bytes accessed | tf_op | source)
XLA Modules:
  0.0 323.2 jit_solution(4221228804349856425)
XLA Ops:
  7.3 23.1 %while.25 = (s32[]{:T(128)}, f32[8,512]{1,0:T(8,128)S(1)}, f32[8,512]{1,0:T(8,128)S(1)}, bf16[8,512,128]{2,1,0:T(8,128)(2,1)}, bf16[2048,128]{1,0:T(8,128)(2,1)}, /*index=5*/s32[]{:T(128)}, s32[]{:T(128)}) while((s32[]{:T(128)}, f32[8,512]{1,0:T(8,128)S(1)}, f32[8,512]{1,0:T(8,128)S(1)}, bf16[8,512,128]{2,1,0:T(8,128)(2,1)}, ...), condition=%wide.region_3.4_spmd, body=%wide.region_0.3_spmd.sunk | while | flops 273677312 | bytes 9058901 | solution.py:33
  7.3 1.9 multiply_reduce_fusion.2
  10.2 1.9 multiply_reduce_fusion.2
  13.0 1.9 multiply_reduce_fusion.2
  15.9 1.9 multiply_reduce_fusion.2
  18.8 1.9 multiply_reduce_fusion.2
  21.7 1.9 multiply_reduce_fusion.2
  24.6 1.9 multiply_reduce_fusion.2
  27.4 1.9 multiply_reduce_fusion.2
  30.3 56.7 %pmax.7 = f32[4096]{0:T(1024)S(1)} all-reduce(f32[4096]{0:T(1024)S(1)} %bitcast.57), channel_id=1, replica_groups=mesh['query'=8,'tok'=16] {'tok'}, use_global_device_ids=true, to_apply=%region_4.5 | all-reduce | flops 4096 | bytes 32768 | tf_op jit(solution)/shard_map/pmax | solution.py:36
  87.0 16.7 %all-gather = f32[65536]{0:T(1024)S(1)} all-gather(f32[4096]{0:T(1024)S(1)} %exponential_multiply_fusion), channel_id=2, replica_groups=mesh['query'=8,'tok'=16] {'tok'}, dimensions={0}, use_global_device_ids=true | all-gather | bytes 278528 | tf_op jit(solution)/shard_map/all_gather | solution.py:38
  104.1 72.0 %while.26 = (s32[]{:T(128)}, f32[2048,128]{1,0:T(8,128)S(1)}, f32[8,512,128]{2,1,0:T(8,128)}, f32[8,512]{1,0:T(8,128)S(1)}, bf16[8,512,128]{2,1,0:T(8,128)(2,1)}...) while((s32[]{:T(128)}, f32[2048,128]{1,0:T(8,128)S(1)}, ...), condition=%wide.region_7.8_spmd.clone, body=%wide.region_6.7_spmd.clone.sunk | while | flops 813236224 | bytes 35145376 | solution.py:58
  109.5 3.6 %convolution_add_fusion.2 = f32[2048,128]{1,0:T(8,128)S(1)} fusion(f32[512,2048]{1,0:T(8,128)} %copy-done, f32[512]{0:T(512)S(1)} %bitcast.53, f32[512]{0:T(512)S(1)} %bitcast.55, f32[2048,128]{1,0:T(8,128)S(1)} %get-tuple-element.237, pred[]{:T(512)S(6)} %compare.3, bf16[8,512,128]{2,1,0:T(8,128)(2,1)} %get-tuple-element.249, s32[]{:T(128)} %get-tuple-element.236), kind=kOutput, calls=%fused_computation.9.clone.1 | convolution fusion | flops 273154048 | bytes 6427137 | tf_op jit(solution)/shard_map/while/body/eval_jaxpr/dot_general | solution.py:53
  118.5 3.6 %convolution_add_fusion.2 = f32[2048,128]{1,0:T(8,128)S(1)} fusion(f32[512,2048]{1,0:T(8,128)} %copy-done, f32[512]{0:T(512)S(1)} %bitcast.53, f32[512]{0:T(512)S(1)} %bitcast.55, f32[2048,128]{1,0:T(8,128)S(1)} %get-tuple-element.237, pred[]{:T(512)S(6)} %compare.3, bf16[8,512,128]{2,1,0:T(8,128)(2,1)} %get-tuple-element.249, s32[]{:T(128)} %get-tuple-element.236), kind=kOutput, calls=%fused_computation.9.clone.1 | convolution fusion | flops 273154048 | bytes 6427137 | tf_op jit(solution)/shard_map/while/body/eval_jaxpr/dot_general | solution.py:53
  127.5 3.6 %convolution_add_fusion.2 = f32[2048,128]{1,0:T(8,128)S(1)} fusion(f32[512,2048]{1,0:T(8,128)} %copy-done, f32[512]{0:T(512)S(1)} %bitcast.53, f32[512]{0:T(512)S(1)} %bitcast.55, f32[2048,128]{1,0:T(8,128)S(1)} %get-tuple-element.237, pred[]{:T(512)S(6)} %compare.3, bf16[8,512,128]{2,1,0:T(8,128)(2,1)} %get-tuple-element.249, s32[]{:T(128)} %get-tuple-element.236), kind=kOutput, calls=%fused_computation.9.clone.1 | convolution fusion | flops 273154048 | bytes 6427137 | tf_op jit(solution)/shard_map/while/body/eval_jaxpr/dot_general | solution.py:53
  133.0 1.9 copy-done
  136.5 3.6 %convolution_add_fusion.2 = f32[2048,128]{1,0:T(8,128)S(1)} fusion(f32[512,2048]{1,0:T(8,128)} %copy-done, f32[512]{0:T(512)S(1)} %bitcast.53, f32[512]{0:T(512)S(1)} %bitcast.55, f32[2048,128]{1,0:T(8,128)S(1)} %get-tuple-element.237, pred[]{:T(512)S(6)} %compare.3, bf16[8,512,128]{2,1,0:T(8,128)(2,1)} %get-tuple-element.249, s32[]{:T(128)} %get-tuple-element.236), kind=kOutput, calls=%fused_computation.9.clone.1 | convolution fusion | flops 273154048 | bytes 6427137 | tf_op jit(solution)/shard_map/while/body/eval_jaxpr/dot_general | solution.py:53
  145.5 3.6 %convolution_add_fusion.2 = f32[2048,128]{1,0:T(8,128)S(1)} fusion(f32[512,2048]{1,0:T(8,128)} %copy-done, f32[512]{0:T(512)S(1)} %bitcast.53, f32[512]{0:T(512)S(1)} %bitcast.55, f32[2048,128]{1,0:T(8,128)S(1)} %get-tuple-element.237, pred[]{:T(512)S(6)} %compare.3, bf16[8,512,128]{2,1,0:T(8,128)(2,1)} %get-tuple-element.249, s32[]{:T(128)} %get-tuple-element.236), kind=kOutput, calls=%fused_computation.9.clone.1 | convolution fusion | flops 273154048 | bytes 6427137 | tf_op jit(solution)/shard_map/while/body/eval_jaxpr/dot_general | solution.py:53
  154.5 3.6 %convolution_add_fusion.2 = f32[2048,128]{1,0:T(8,128)S(1)} fusion(f32[512,2048]{1,0:T(8,128)} %copy-done, f32[512]{0:T(512)S(1)} %bitcast.53, f32[512]{0:T(512)S(1)} %bitcast.55, f32[2048,128]{1,0:T(8,128)S(1)} %get-tuple-element.237, pred[]{:T(512)S(6)} %compare.3, bf16[8,512,128]{2,1,0:T(8,128)(2,1)} %get-tuple-element.249, s32[]{:T(128)} %get-tuple-element.236), kind=kOutput, calls=%fused_computation.9.clone.1 | convolution fusion | flops 273154048 | bytes 6427137 | tf_op jit(solution)/shard_map/while/body/eval_jaxpr/dot_general | solution.py:53
  160.0 1.9 copy-done
  163.5 3.6 %convolution_add_fusion.2 = f32[2048,128]{1,0:T(8,128)S(1)} fusion(f32[512,2048]{1,0:T(8,128)} %copy-done, f32[512]{0:T(512)S(1)} %bitcast.53, f32[512]{0:T(512)S(1)} %bitcast.55, f32[2048,128]{1,0:T(8,128)S(1)} %get-tuple-element.237, pred[]{:T(512)S(6)} %compare.3, bf16[8,512,128]{2,1,0:T(8,128)(2,1)} %get-tuple-element.249, s32[]{:T(128)} %get-tuple-element.236), kind=kOutput, calls=%fused_computation.9.clone.1 | convolution fusion | flops 273154048 | bytes 6427137 | tf_op jit(solution)/shard_map/while/body/eval_jaxpr/dot_general | solution.py:53
  172.5 3.6 %convolution_add_fusion.2 = f32[2048,128]{1,0:T(8,128)S(1)} fusion(f32[512,2048]{1,0:T(8,128)} %copy-done, f32[512]{0:T(512)S(1)} %bitcast.53, f32[512]{0:T(512)S(1)} %bitcast.55, f32[2048,128]{1,0:T(8,128)S(1)} %get-tuple-element.237, pred[]{:T(512)S(6)} %compare.3, bf16[8,512,128]{2,1,0:T(8,128)(2,1)} %get-tuple-element.249, s32[]{:T(128)} %get-tuple-element.236), kind=kOutput, calls=%fused_computation.9.clone.1 | convolution fusion | flops 273154048 | bytes 6427137 | tf_op jit(solution)/shard_map/while/body/eval_jaxpr/dot_general | solution.py:53
  177.9 72.0 %reduce-scatter.5.cloned.1.call-done = f32[256,128]{1,0:T(8,128)} async-done(((f32[2048,128]{1,0:T(8,128)}), f32[256,128]{1,0:T(8,128)}) %reduce-scatter.5.cloned.1.call-update) | async-done | bytes 131088 | tf_op jit(solution)/shard_map/reduce_scatter | solution.py:63
  249.9 66.4 %reduce-scatter.3.cloned.1.call-done = f32[256,128]{1,0:T(8,128)} async-done(((f32[4096,128]{1,0:T(8,128)}), f32[256,128]{1,0:T(8,128)}) %reduce-scatter.3.cloned.1.call-update) | async-done | bytes 131088 | tf_op jit(solution)/shard_map/reduce_scatter | solution.py:65
  (100 shorter events, 48.6 us)
Async XLA Ops:
  7.2 242.8 %reduce-scatter.5.cloned.1.call-start = ((), (), s32[]{:S(2)}) async-start(), calls=%async_computation.3 | async-start | bytes 1179648 | tf_op jit(solution)/shard_map/reduce_scatter | solution.py:63
  7.2 96.6 %copy-start.3 = (f32[128]{0:T(128)S(1)}, f32[128]{0:T(128)}, u32[]{:S(2)}) copy-start(f32[128]{0:T(128)} %param.9) | copy-start | bytes 1540
  104.1 3.8 %copy-start.1 = (bf16[2048,128]{1,0:T(8,128)(2,1)S(1)}, bf16[2048,128]{1,0:T(8,128)(2,1)}, u32[]{:S(2)}) copy-start(bf16[2048,128]{1,0:T(8,128)(2,1)} %get-tuple-element.250) | copy-start | bytes 1572868 | tf_op jit(solution)/shard_map/while
  106.0 1.9 copy-start
  113.1 3.8 %copy-start.1 = (bf16[2048,128]{1,0:T(8,128)(2,1)S(1)}, bf16[2048,128]{1,0:T(8,128)(2,1)}, u32[]{:S(2)}) copy-start(bf16[2048,128]{1,0:T(8,128)(2,1)} %get-tuple-element.250) | copy-start | bytes 1572868 | tf_op jit(solution)/shard_map/while
  115.0 1.9 copy-start
  122.1 3.8 %copy-start.1 = (bf16[2048,128]{1,0:T(8,128)(2,1)S(1)}, bf16[2048,128]{1,0:T(8,128)(2,1)}, u32[]{:S(2)}) copy-start(bf16[2048,128]{1,0:T(8,128)(2,1)} %get-tuple-element.250) | copy-start | bytes 1572868 | tf_op jit(solution)/shard_map/while
  124.0 1.9 copy-start
  131.1 3.8 %copy-start.1 = (bf16[2048,128]{1,0:T(8,128)(2,1)S(1)}, bf16[2048,128]{1,0:T(8,128)(2,1)}, u32[]{:S(2)}) copy-start(bf16[2048,128]{1,0:T(8,128)(2,1)} %get-tuple-element.250) | copy-start | bytes 1572868 | tf_op jit(solution)/shard_map/while
  133.0 1.9 copy-start
  140.1 3.8 %copy-start.1 = (bf16[2048,128]{1,0:T(8,128)(2,1)S(1)}, bf16[2048,128]{1,0:T(8,128)(2,1)}, u32[]{:S(2)}) copy-start(bf16[2048,128]{1,0:T(8,128)(2,1)} %get-tuple-element.250) | copy-start | bytes 1572868 | tf_op jit(solution)/shard_map/while
  142.0 1.9 copy-start
  149.1 3.8 %copy-start.1 = (bf16[2048,128]{1,0:T(8,128)(2,1)S(1)}, bf16[2048,128]{1,0:T(8,128)(2,1)}, u32[]{:S(2)}) copy-start(bf16[2048,128]{1,0:T(8,128)(2,1)} %get-tuple-element.250) | copy-start | bytes 1572868 | tf_op jit(solution)/shard_map/while
  151.0 1.9 copy-start
  158.1 3.8 %copy-start.1 = (bf16[2048,128]{1,0:T(8,128)(2,1)S(1)}, bf16[2048,128]{1,0:T(8,128)(2,1)}, u32[]{:S(2)}) copy-start(bf16[2048,128]{1,0:T(8,128)(2,1)} %get-tuple-element.250) | copy-start | bytes 1572868 | tf_op jit(solution)/shard_map/while
  160.0 1.9 copy-start
  167.1 3.8 %copy-start.1 = (bf16[2048,128]{1,0:T(8,128)(2,1)S(1)}, bf16[2048,128]{1,0:T(8,128)(2,1)}, u32[]{:S(2)}) copy-start(bf16[2048,128]{1,0:T(8,128)(2,1)} %get-tuple-element.250) | copy-start | bytes 1572868 | tf_op jit(solution)/shard_map/while
  169.0 1.9 copy-start
  176.1 1.0 copy-start.2
  177.1 139.2 %reduce-scatter.3.cloned.1.call-start = ((), (), s32[]{:S(2)}) async-start(), calls=%async_computation.2 | async-start | bytes 2228224 | tf_op jit(solution)/shard_map/reduce_scatter | solution.py:65
Sparse Core Ops, SparseCore 0:
  177.2 72.6 reduce-scatter.4
  252.9 63.4 reduce-scatter.2
